TPU v7x, 32 devices: a whole 2x2x4 slice. The times are simulated.
32 devices in a mesh: dp: 8 (over z, x), seq: 4 (over y, core).
Axes of the slice: x: 2, y: 2, z: 4, core: 2. Of those that a mesh axis runs over, the one named last changes fastest.
Arguments:
- hidden_states: bfloat16 [8, 2, 1024, 1024], P('dp', None, 'seq'), may hold values from -8.5 to 8.5
- lengths: int32 [8, 2], P('dp'), may hold values from 256 to 1024, as said below
- w_query: bfloat16 [1024, 1024], replicated, may hold values from -0.1875 to 0.1875
- w_key: bfloat16 [1024, 1024], replicated, may hold values from -0.1875 to 0.1875
- w_value: bfloat16 [1024, 1024], replicated, may hold values from -0.1875 to 0.1875
- w_out: bfloat16 [1024, 1024], replicated, may hold values from -0.1875 to 0.1875
- running_cov: float32 [1024, 1024], P('seq'), as said below
Outputs:
- whitened: float32 [8, 2, 1024], P('dp')
- cov_new: float32 [1024, 1024], P('seq')
- loss: float32 [], replicated
Inputs may be any that keep to these rules, and one draw needn't show every extreme that they name: `lengths`: at least a quarter of a module is valid; some module has all 1024 tokens valid. `running_cov`: Symmetric, with a diagonal larger than the sum of the magnitudes of its row's other entries.
All inputs are finite; a program needn't handle non-finite values.
Results may differ from a plain program's by a relative error of at most 0.0037.
The roundings to bfloat16 on the way count: a program that leaves them out, or rounds other values in their place, can miss the bound.
Values sent between devices are 32-bit elements; how exact they have to be, the bound alone decides.
No kernel may reach another device: no remote copies, remote signals or barrier semaphores. Data moves between devices by JAX's collectives and lax.ppermute only.
A program may use at most 128 MiB of HBM per device.

v0:
```python
import jax
import jax.numpy as jnp
from jax import lax
from jax.sharding import PartitionSpec as P

HEADS = 16
HEAD_DIM = 64


def passed_along(array, axis, by):
    size = lax.axis_size(axis)
    pairs = [(i, i + by) for i in range(size) if 0 <= i + by < size]
    return lax.ppermute(array, axis, pairs)


def feature(u):
    return jnp.where(u > 0.0, u + 1.0, jnp.exp(jnp.minimum(u, 0.0)))


def whiten_rows(full_cov, sum_embed, second, total, rows_in):
    mean = sum_embed / total
    batch_cov = (second - total * mean[:, None] * mean[None, :]) / (total - 1)
    cov_full = 0.5 * full_cov + 0.5 * batch_cov
    chol = jnp.linalg.cholesky(cov_full)
    result = lax.linalg.triangular_solve(chol, (rows_in - mean).T, left_side=True, lower=True).T
    return (cov_full, result)


def pair_terms(whitened_rows):
    normed = whitened_rows / jnp.sqrt(
        jnp.sum(whitened_rows * whitened_rows, axis=1, keepdims=True) + 1e-06
    )
    normed = normed.reshape(-1, 2, normed.shape[1])
    gap = normed[:, 0] - normed[:, 1]
    return jnp.sum(gap * gap)


def body(hidden_states, lengths, w_query, w_key, w_value, w_out, running_cov):
    pairs, two, span, width = hidden_states.shape
    count = pairs * two
    heads = HEADS
    head_dim = HEAD_DIM
    rows = hidden_states.reshape(count * span, width)

    def project(weight):
        return jnp.dot(rows, weight, preferred_element_type=jnp.float32)

    f_query = feature(project(w_query)).astype(jnp.bfloat16).reshape(count, span, heads, head_dim)
    f_key = feature(project(w_key)).astype(jnp.bfloat16).reshape(count, span, heads, head_dim)
    values = project(w_value).astype(jnp.bfloat16).reshape(count, span, heads, head_dim)
    local_state = jnp.einsum("slhe,slhf->shef", f_key, values, preferred_element_type=jnp.float32)
    local_norm = jnp.sum(f_key.astype(jnp.float32), axis=1)
    empty_state = jnp.zeros_like(local_state)
    empty_norm = jnp.zeros_like(local_norm)

    def relay(step, carried):
        return passed_along((carried[0] + local_state, carried[1] + local_norm), "seq", 1)

    prior_state, prior_norm = lax.fori_loop(
        0, lax.axis_size("seq") - 1, relay, (empty_state, empty_norm)
    )
    scores = jnp.einsum("slhe,smhe->shlm", f_query, f_key, preferred_element_type=jnp.float32)
    causal = jnp.arange(span)[:, None] >= jnp.arange(span)[None, :]
    scores = jnp.where(causal, scores, 0.0)
    weights = scores.astype(jnp.bfloat16)
    numer = jnp.einsum("shlm,smhf->slhf", weights, values, preferred_element_type=jnp.float32)
    numer = numer + jnp.einsum(
        "slhe,shef->slhf",
        f_query,
        prior_state.astype(jnp.bfloat16),
        preferred_element_type=jnp.float32,
    )
    denom = jnp.transpose(jnp.sum(scores, axis=-1), (0, 2, 1))
    denom = denom + jnp.einsum("slhe,she->slh", f_query.astype(jnp.float32), prior_norm)
    attended = (numer / denom[..., None]).astype(jnp.bfloat16).reshape(count * span, width)
    layer_out = rows.astype(jnp.float32) + jnp.dot(
        attended, w_out, preferred_element_type=jnp.float32
    )
    position = lax.axis_index("seq") * span + jnp.arange(span)
    flat_len = lengths.reshape(count)
    valid = (position[None, :] < flat_len[:, None]).astype(jnp.float32)
    pooled = jnp.sum(layer_out.reshape(count, span, width) * valid[:, :, None], axis=1)
    pooled = lax.psum(pooled, "seq")
    embed = pooled / flat_len[:, None].astype(jnp.float32)
    full_cov = lax.all_gather(running_cov, "seq", axis=0, tiled=True)
    total = lax.axis_size("dp") * count
    own_outer = jnp.dot(
        embed.T, embed, precision=lax.Precision.HIGHEST, preferred_element_type=jnp.float32
    )
    sum_embed, second = lax.psum((jnp.sum(embed, axis=0), own_outer), "dp")
    cov_full, whitened = whiten_rows(full_cov, sum_embed, second, total, embed)
    loss = lax.psum(pair_terms(whitened), "dp") / (pairs * lax.axis_size("dp"))
    share = running_cov.shape[0]
    cov_rows = lax.dynamic_slice_in_dim(cov_full, lax.axis_index("seq") * share, share, 0)
    return (whitened.reshape(pairs, two, width), cov_rows, loss)


def solution(mesh):
    placed = (P("dp", None, "seq", None), P("dp", None), P(), P(), P(), P(), P("seq", None))
    return jax.shard_map(
        body,
        mesh=mesh,
        in_specs=placed,
        out_specs=(P("dp", None, None), P("seq", None), P()),
        check_vma=False,
    )
```

profile of v0, /device:TPU:0, one launch (start us, length us, event | category | flops | bytes accessed | tf_op | source)
XLA Modules:
  0.0 632.7 jit_solution(18064278824719180027)
XLA Ops:
  32.5 41.2 %while.13 = (s32[]{:T(128)}, f32[2,16,64,64]{3,2,1,0:T(8,128)S(1)}, f32[2,16,64]{2,1,0:T(8,128)S(1)}, f32[2,16,64,64]{3,2,1,0:T(8,128)S(1)}, f32[2,16,64]{2,1,0:T(8,128)S(1)}, /*index=5*/s32[]{:T(128)}) while((s32[]{:T(128)}, f32[2,16,64,64]{3,2,1,0:T(8,128)S(1)}, f32[2,16,64]{2,1,0:T(8,128)S(1)}, f32[2,16,64,64]{3,2,1,0:T(8,128)S(1)}, ...), condition=%wide.region_2.3_spmd, body=%wide.region_1.2_spmd.sunk | while | flops 133122 | bytes 3727509 | solution.py:59
  35.1 4.5 collective-permute-start.1
  40.5 11.1 %collective-permute-start = (f32[2,16,64,64]{3,2,1,0:T(8,128)S(1)}, f32[2,16,64,64]{3,2,1,0:T(8,128)S(1)}, u32[]{:S(2)}, u32[]{:S(2)}) collective-permute-start(f32[2,16,64,64]{3,2,1,0:T(8,128)S(1)} %add.171), channel_id=1, source_target_pairs={{0,1},{1,2},{2,3},{4,5},{5,6},{6,7},{8,9},{9,10},{10,11},{12,13},{... | collective-permute-start | bytes 1572872 | tf_op jit(solution)/shard_map/while/body/eval_jaxpr/ppermute | solution.py:13
  51.7 4.3 collective-permute-start.1
  57.0 11.1 %collective-permute-start = (f32[2,16,64,64]{3,2,1,0:T(8,128)S(1)}, f32[2,16,64,64]{3,2,1,0:T(8,128)S(1)}, u32[]{:S(2)}, u32[]{:S(2)}) collective-permute-start(f32[2,16,64,64]{3,2,1,0:T(8,128)S(1)} %add.171), channel_id=1, source_target_pairs={{0,1},{1,2},{2,3},{4,5},{5,6},{6,7},{8,9},{9,10},{10,11},{12,13},{... | collective-permute-start | bytes 1572872 | tf_op jit(solution)/shard_map/while/body/eval_jaxpr/ppermute | solution.py:13
  68.1 4.3 collective-permute-start.1
  82.6 15.1 %psum.28 = f32[2,1024]{1,0:T(2,128)S(1)} all-reduce(f32[2,1024]{1,0:T(2,128)S(1)} %multiply_reduce_fusion), channel_id=1, replica_groups=mesh['dp'=8,'seq'=4] {'seq'}, use_global_device_ids=true, to_apply=%region_5.6 | all-reduce | flops 2048 | bytes 16384 | tf_op jit(solution)/shard_map/psum | solution.py:83
  97.8 5.1 fusion.80
  103.5 22.2 %psum.30 = f32[1024]{0:T(1024)S(1)} all-reduce(f32[1024]{0:T(1024)S(1)} %get-tuple-element.64), channel_id=1, replica_groups=mesh['dp'=8,'seq'=4] {'dp'}, use_global_device_ids=true, to_apply=%region_8.9 | all-reduce | flops 1024 | bytes 8192 | tf_op jit(solution)/shard_map/psum | solution.py:90
  125.7 135.8 %all-reduce.3.cloned.1.call-done = f32[1024,1024]{1,0:T(8,128)} async-done(((f32[1024,1024]{1,0:T(8,128)}), f32[1024,1024]{1,0:T(8,128)}) %all-reduce.3.cloned.1.call-update) | async-done | bytes 4194320 | tf_op jit(solution)/shard_map/psum | solution.py:90
  261.5 6.2 multiply_add_fusion
  267.7 5.5 copy.45
  273.2 4.4 fusion.1
  279.6 11.7 %cholesky.223 = f32[128,128]{1,0:T(8,128)S(1)} custom-call(f32[128,128]{1,0:T(8,128)S(1)} %cholesky.580), custom_call_target="Cholesky" | custom-call | tf_op jit(solution)/shard_map/jit(cholesky)/cholesky | solution.py:24
  293.8 9.8 %custom-call.62 = f32[1,128,128]{1,2,0:T(8,128)S(1)} custom-call(f32[1,128,128]{2,1,0:T(8,128)S(1)} %get-tuple-element.89), custom_call_target="InvertDiagBlocksLowerTriangular" | custom-call | tf_op jit(solution)/shard_map/jit(cholesky)/cholesky | solution.py:24
  307.6 11.9 %cholesky.244 = f32[128,128]{1,0:T(8,128)S(1)} custom-call(f32[128,128]{1,0:T(8,128)S(1)} %cholesky.584), custom_call_target="Cholesky" | custom-call | tf_op jit(solution)/shard_map/jit(cholesky)/cholesky | solution.py:24
  320.1 9.8 %custom-call.63 = f32[1,128,128]{1,2,0:T(8,128)S(1)} custom-call(f32[1,128,128]{2,1,0:T(8,128)S(1)} %get-tuple-element.86), custom_call_target="InvertDiagBlocksLowerTriangular" | custom-call | tf_op jit(solution)/shard_map/jit(cholesky)/cholesky | solution.py:24
  333.3 11.7 %cholesky.468 = f32[128,128]{1,0:T(8,128)S(1)} custom-call(f32[128,128]{1,0:T(8,128)S(1)} %cholesky.589), custom_call_target="Cholesky" | custom-call | tf_op jit(solution)/shard_map/jit(cholesky)/cholesky | solution.py:24
  346.3 9.8 %custom-call.64 = f32[1,128,128]{1,2,0:T(8,128)S(1)} custom-call(f32[1,128,128]{2,1,0:T(8,128)S(1)} %get-tuple-element.83), custom_call_target="InvertDiagBlocksLowerTriangular" | custom-call | tf_op jit(solution)/shard_map/jit(cholesky)/cholesky | solution.py:24
  359.7 12.1 %cholesky.487 = f32[128,128]{1,0:T(8,128)S(1)} custom-call(f32[128,128]{1,0:T(8,128)S(1)} %cholesky.594), custom_call_target="Cholesky" | custom-call | tf_op jit(solution)/shard_map/jit(cholesky)/cholesky | solution.py:24
  373.1 9.8 %custom-call.65 = f32[1,128,128]{1,2,0:T(8,128)S(1)} custom-call(f32[1,128,128]{2,1,0:T(8,128)S(1)} %get-tuple-element.80), custom_call_target="InvertDiagBlocksLowerTriangular" | custom-call | tf_op jit(solution)/shard_map/jit(cholesky)/cholesky | solution.py:24
  386.4 11.7 %cholesky.506 = f32[128,128]{1,0:T(8,128)S(1)} custom-call(f32[128,128]{1,0:T(8,128)S(1)} %cholesky.599), custom_call_target="Cholesky" | custom-call | tf_op jit(solution)/shard_map/jit(cholesky)/cholesky | solution.py:24
  399.5 9.9 %custom-call.66 = f32[1,128,128]{1,2,0:T(8,128)S(1)} custom-call(f32[1,128,128]{2,1,0:T(8,128)S(1)} %get-tuple-element.77), custom_call_target="InvertDiagBlocksLowerTriangular" | custom-call | tf_op jit(solution)/shard_map/jit(cholesky)/cholesky | solution.py:24
  412.7 11.7 %cholesky.526 = f32[128,128]{1,0:T(8,128)S(1)} custom-call(f32[128,128]{1,0:T(8,128)S(1)} %cholesky.604), custom_call_target="Cholesky" | custom-call | tf_op jit(solution)/shard_map/jit(cholesky)/cholesky | solution.py:24
  425.8 9.8 %custom-call.67 = f32[1,128,128]{1,2,0:T(8,128)S(1)} custom-call(f32[1,128,128]{2,1,0:T(8,128)S(1)} %get-tuple-element.74), custom_call_target="InvertDiagBlocksLowerTriangular" | custom-call | tf_op jit(solution)/shard_map/jit(cholesky)/cholesky | solution.py:24
  438.6 11.9 %cholesky.546 = f32[128,128]{1,0:T(8,128)S(1)} custom-call(f32[128,128]{1,0:T(8,128)S(1)} %cholesky.609), custom_call_target="Cholesky" | custom-call | tf_op jit(solution)/shard_map/jit(cholesky)/cholesky | solution.py:24
  451.8 9.8 %custom-call.68 = f32[1,128,128]{1,2,0:T(8,128)S(1)} custom-call(f32[1,128,128]{2,1,0:T(8,128)S(1)} %get-tuple-element.71), custom_call_target="InvertDiagBlocksLowerTriangular" | custom-call | tf_op jit(solution)/shard_map/jit(cholesky)/cholesky | solution.py:24
  464.3 11.7 %cholesky.564 = f32[128,128]{1,0:T(8,128)S(1)} custom-call(f32[128,128]{1,0:T(8,128)S(1)} %convolution_subtract_fusion.6), custom_call_target="Cholesky" | custom-call | tf_op jit(solution)/shard_map/jit(cholesky)/cholesky | solution.py:24
  483.1 5.0 select_select_fusion
  488.0 23.2 %while.14 = (s32[]{:T(128)}, f32[1024,1024]{1,0:T(8,128)}, s32[8,2]{0,1:T(2,128)S(1)}, f32[8,128,128]{2,1,0:T(8,128)S(1)}, s32[]{:T(128)}) while((s32[]{:T(128)}, f32[1024,1024]{1,0:T(8,128)}, s32[8,2]{0,1:T(2,128)S(1)}, f32[8,128,128]{2,1,0:T(8,128)S(1)}, s32[]{:T(128)}) %tuple.81), condition=%wide.while_cond, body=%wide.while_body.sunk | while | flops 2 | bytes 131189 | solution.py:25
  511.2 78.6 %custom-call.69 = f32[8,128,128]{1,2,0:T(8,128)S(1)} custom-call(f32[8,128,128]{2,1,0:T(8,128)S(1)} %get-tuple-element.40), custom_call_target="InvertDiagBlocksLowerTriangular" | custom-call | tf_op jit(solution)/shard_map/triangular_solve | solution.py:25
  603.5 19.7 %psum.31 = f32[]{:T(128)} all-reduce(f32[]{:T(128)} %fusion.63), channel_id=1, replica_groups=mesh['dp'=8,'seq'=4] {'dp'}, use_global_device_ids=true, to_apply=%region_27.28 | all-reduce | flops 1 | bytes 8 | tf_op jit(solution)/shard_map/psum | solution.py:92
  (157 shorter events, 112.7 us)
Async XLA Ops:
  8.0 1.6 copy-start
  8.0 253.5 %all-reduce.3.cloned.1.call-start = ((), (), s32[]{:S(2)}) async-start(), calls=%async_computation.1 | async-start | bytes 8388608 | tf_op jit(solution)/shard_map/psum | solution.py:90
  12.8 1.7 copy-start.9
  13.1 18.4 %copy-start.3 = (bf16[2,256,16,64]{1,0,3,2:T(2,128)(2,1)}, bf16[2,256,16,64]{1,0,3,2:T(2,128)(2,1)S(1)}, u32[]{:S(2)}) copy-start(bf16[2,256,16,64]{1,0,3,2:T(2,128)(2,1)S(1)} %reshape.179) | copy-start | bytes 3145732
  31.5 1.0 copy-start.6
  32.6 7.7 %collective-permute-start = (f32[2,16,64,64]{3,2,1,0:T(8,128)S(1)}, f32[2,16,64,64]{3,2,1,0:T(8,128)S(1)}, u32[]{:S(2)}, u32[]{:S(2)}) collective-permute-start(f32[2,16,64,64]{3,2,1,0:T(8,128)S(1)} %add.171), channel_id=1, source_target_pairs={{0,1},{1,2},{2,3},{4,5},{5,6},{6,7},{8,9},{9,10},{10,11},{12,13},{... | collective-permute-start | bytes 1572872 | tf_op jit(solution)/shard_map/while/body/eval_jaxpr/ppermute | solution.py:13
  35.1 5.3 collective-permute-start.1
  40.5 16.3 %collective-permute-start = (f32[2,16,64,64]{3,2,1,0:T(8,128)S(1)}, f32[2,16,64,64]{3,2,1,0:T(8,128)S(1)}, u32[]{:S(2)}, u32[]{:S(2)}) collective-permute-start(f32[2,16,64,64]{3,2,1,0:T(8,128)S(1)} %add.171), channel_id=1, source_target_pairs={{0,1},{1,2},{2,3},{4,5},{5,6},{6,7},{8,9},{9,10},{10,11},{12,13},{... | collective-permute-start | bytes 1572872 | tf_op jit(solution)/shard_map/while/body/eval_jaxpr/ppermute | solution.py:13
  51.7 5.2 collective-permute-start.1
  57.0 16.3 %collective-permute-start = (f32[2,16,64,64]{3,2,1,0:T(8,128)S(1)}, f32[2,16,64,64]{3,2,1,0:T(8,128)S(1)}, u32[]{:S(2)}, u32[]{:S(2)}) collective-permute-start(f32[2,16,64,64]{3,2,1,0:T(8,128)S(1)} %add.171), channel_id=1, source_target_pairs={{0,1},{1,2},{2,3},{4,5},{5,6},{6,7},{8,9},{9,10},{10,11},{12,13},{... | collective-permute-start | bytes 1572872 | tf_op jit(solution)/shard_map/while/body/eval_jaxpr/ppermute | solution.py:13
  68.1 5.2 collective-permute-start.1
  73.7 3.4 copy-start.4
  73.7 3.4 copy-start.5
  77.1 1.4 copy-start.7
  79.4 1.4 copy-start.12
  79.4 1.6 copy-start.8
  79.4 1.9 copy-start.10
  102.9 158.6 %all-gather.2.cloned.1.call-start = ((), (), s32[]{:S(2)}) async-start(), calls=%async_computation | async-start | bytes 5242880 | tf_op jit(solution)/shard_map/all_gather | solution.py:85
  277.6 2.0 copy-start.2
  483.0 140.8 %copy-start.1 = (bf16[1024,1024]{1,0:T(8,128)(2,1)S(1)}, bf16[1024,1024]{1,0:T(8,128)(2,1)}, u32[]{:S(2)}) copy-start(bf16[1024,1024]{1,0:T(8,128)(2,1)} %param.12) | copy-start | bytes 6291460
  600.3 23.5 %copy-start.11 = (f32[1024,2]{0,1:T(2,128)}, f32[1024,2]{0,1:T(2,128)S(1)}, u32[]{:S(2)}) copy-start(f32[1024,2]{0,1:T(2,128)S(1)} %convolution_dynamic-update-slice_fusion.6) | copy-start | bytes 24580
Sparse Core Ops, SparseCore 0:
  103.0 158.4 all-reduce.2
Sparse Core Ops, SparseCore 1:
  104.9 36.3 all-gather.1
where the time goes:
time: 641 us; the launch traced here: 633 us
  other arithmetic  270 us (42%)
  waiting for transfers between devices  139 us (22%)
  blocking collectives  57 us (9%)
  matrix products  54.5 us (9%)
  local copies, waits for them, and re-layouts  50.5 us (8%)
  starting transfers between devices  37.9 us (6%)
  between operations  23.1 us (4%)
    another operation x30, other arithmetic, whiten_rows(): chol = jnp.linalg.cholesky(cov_full)  173 us
    psum x1, waiting for transfers between devices, body(): sum_embed, second = lax.psum((jnp.sum(embed, axis=0), own_outer), 'dp')  136 us
    another operation x3, other arithmetic, whiten_rows(): lax.linalg.triangular_solve(chol, (rows_in - mean).T, left_side=True, low...  83.6 us
    ppermute x6, starting transfers between devices, passed_along(): return lax.ppermute(array, axis, pairs)  37.8 us
    another operation x14, matrix products, whiten_rows(): chol = jnp.linalg.cholesky(cov_full)  23.1 us
    another operation x24, local copies, waits for them, and re-layouts  23 us
    psum x1, blocking collectives, body(): sum_embed, second = lax.psum((jnp.sum(embed, axis=0), own_outer), 'dp')  22.2 us
    psum x1, blocking collectives, body(): loss = lax.psum(pair_terms(whitened), 'dp') / (pairs * lax.axis_size('dp'))  19.7 us
  transfers between devices with their start and end apart: 8, of which 4 were waited for; matrix products, arithmetic and copies ran while one was open for 0% of the time, Pallas kernels for 0%

commit v1 on v0

--- a/solution.py
+++ b/solution.py
@@ -80,7 +80,9 @@
     flat_len = lengths.reshape(count)
     valid = (position[None, :] < flat_len[:, None]).astype(jnp.float32)
     pooled = jnp.sum(layer_out.reshape(count, span, width) * valid[:, :, None], axis=1)
-    pooled = lax.psum(pooled, "seq")
+    pooled = pooled
+    for hop in (1, 2):
+        pooled = pooled + lax.ppermute(pooled, "seq", [(dev, dev ^ hop) for dev in range(4)])
     embed = pooled / flat_len[:, None].astype(jnp.float32)
     full_cov = lax.all_gather(running_cov, "seq", axis=0, tiled=True)
     total = lax.axis_size("dp") * count

time: 641 us -> 640 us (level)
  blocking collectives: 57 us -> 42.1 us
  starting transfers between devices: 37.9 us -> 49.8 us
    psum x1 -> x0, blocking collectives: 15.1 us -> none  [body(): pooled = lax.psum(pooled, 'seq')]
    ppermute x0 -> x2, starting transfers between devices: none -> 11.9 us  [body(): lax.ppermute(pooled, 'seq', [(dev, dev ^ hop) for dev in range(4)])]
  transfers between devices with their start and end apart: 8 -> 10, of which waited for: 4 -> 6; matrix products, arithmetic and copies ran while one was open for 0% -> 0% of each run, Pallas kernels for 0% -> 0%
where the time goes in v1:
time: 640 us; the launch traced here: 632 us
  other arithmetic  269 us (42%)
  waiting for transfers between devices  141 us (22%)
  matrix products  54.5 us (9%)
  local copies, waits for them, and re-layouts  51.3 us (8%)
  starting transfers between devices  49.8 us (8%)
  blocking collectives  42.1 us (7%)
  between operations  23.1 us (4%)
    another operation x30, other arithmetic, whiten_rows(): chol = jnp.linalg.cholesky(cov_full)  173 us
    psum x1, waiting for transfers between devices, body(): sum_embed, second = lax.psum((jnp.sum(embed, axis=0), own_outer), 'dp')  135 us
    another operation x3, other arithmetic, whiten_rows(): lax.linalg.triangular_solve(chol, (rows_in - mean).T, left_side=True, low...  83.6 us
    ppermute x6, starting transfers between devices, passed_along(): return lax.ppermute(array, axis, pairs)  37.8 us
    another operation x14, matrix products, whiten_rows(): chol = jnp.linalg.cholesky(cov_full)  23.1 us
    another operation x24, local copies, waits for them, and re-layouts  23 us
    psum x1, blocking collectives, body(): sum_embed, second = lax.psum((jnp.sum(embed, axis=0), own_outer), 'dp')  22.4 us
    psum x1, blocking collectives, body(): loss = lax.psum(pair_terms(whitened), 'dp') / (pairs * lax.axis_size('dp'))  19.7 us
  transfers between devices with their start and end apart: 10, of which 6 were waited for; matrix products, arithmetic and copies ran while one was open for 0% of the time, Pallas kernels for 0%

profile of v1, /device:TPU:0, one launch (start us, length us, event | category | flops | bytes accessed | tf_op | source)
XLA Modules:
  0.0 631.6 jit_solution(9357885682753353353)
XLA Ops:
  32.5 41.2 %while.13 = (s32[]{:T(128)}, f32[2,16,64,64]{3,2,1,0:T(8,128)S(1)}, f32[2,16,64]{2,1,0:T(8,128)S(1)}, f32[2,16,64,64]{3,2,1,0:T(8,128)S(1)}, f32[2,16,64]{2,1,0:T(8,128)S(1)}, /*index=5*/s32[]{:T(128)}) while((s32[]{:T(128)}, f32[2,16,64,64]{3,2,1,0:T(8,128)S(1)}, f32[2,16,64]{2,1,0:T(8,128)S(1)}, f32[2,16,64,64]{3,2,1,0:T(8,128)S(1)}, ...), condition=%wide.region_2.3_spmd, body=%wide.region_1.2_spmd.sunk | while | flops 133122 | bytes 3727509 | solution.py:59
  35.1 4.5 collective-permute-start.1
  40.5 11.1 %collective-permute-start = (f32[2,16,64,64]{3,2,1,0:T(8,128)S(1)}, f32[2,16,64,64]{3,2,1,0:T(8,128)S(1)}, u32[]{:S(2)}, u32[]{:S(2)}) collective-permute-start(f32[2,16,64,64]{3,2,1,0:T(8,128)S(1)} %add.179), channel_id=1, source_target_pairs={{0,1},{1,2},{2,3},{4,5},{5,6},{6,7},{8,9},{9,10},{10,11},{12,13},{... | collective-permute-start | bytes 1572872 | tf_op jit(solution)/shard_map/while/body/eval_jaxpr/ppermute | solution.py:13
  51.7 4.3 collective-permute-start.1
  57.0 11.1 %collective-permute-start = (f32[2,16,64,64]{3,2,1,0:T(8,128)S(1)}, f32[2,16,64,64]{3,2,1,0:T(8,128)S(1)}, u32[]{:S(2)}, u32[]{:S(2)}) collective-permute-start(f32[2,16,64,64]{3,2,1,0:T(8,128)S(1)} %add.179), channel_id=1, source_target_pairs={{0,1},{1,2},{2,3},{4,5},{5,6},{6,7},{8,9},{9,10},{10,11},{12,13},{... | collective-permute-start | bytes 1572872 | tf_op jit(solution)/shard_map/while/body/eval_jaxpr/ppermute | solution.py:13
  68.1 4.3 collective-permute-start.1
  82.6 9.2 %collective-permute-start.2 = (f32[2,1024]{1,0:T(2,128)S(1)}, f32[2,1024]{1,0:T(2,128)S(1)}, u32[]{:S(2)}, u32[]{:S(2)}) collective-permute-start(f32[2,1024]{1,0:T(2,128)S(1)} %multiply_reduce_fusion), channel_id=1, source_target_pairs={{0,1},{1,0},{2,3},{3,2},{4,5},{5,4},{6,7},{7,6},{8,9},{9,8},{10,11... | collective-permute-start | bytes 24584 | tf_op jit(solution)/shard_map/ppermute | solution.py:85
  97.0 5.1 fusion.87
  102.7 22.4 %psum.22 = f32[1024]{0:T(1024)S(1)} all-reduce(f32[1024]{0:T(1024)S(1)} %get-tuple-element.64), channel_id=1, replica_groups=mesh['dp'=8,'seq'=4] {'dp'}, use_global_device_ids=true, to_apply=%region_7.8 | all-reduce | flops 1024 | bytes 8192 | tf_op jit(solution)/shard_map/psum | solution.py:92
  125.2 135.3 %all-reduce.3.cloned.1.call-done = f32[1024,1024]{1,0:T(8,128)} async-done(((f32[1024,1024]{1,0:T(8,128)}), f32[1024,1024]{1,0:T(8,128)}) %all-reduce.3.cloned.1.call-update) | async-done | bytes 4194320 | tf_op jit(solution)/shard_map/psum | solution.py:92
  260.5 6.2 multiply_add_fusion
  266.6 5.5 copy.45
  272.1 4.4 fusion.1
  278.5 11.7 %cholesky.223 = f32[128,128]{1,0:T(8,128)S(1)} custom-call(f32[128,128]{1,0:T(8,128)S(1)} %cholesky.580), custom_call_target="Cholesky" | custom-call | tf_op jit(solution)/shard_map/jit(cholesky)/cholesky | solution.py:24
  292.8 9.8 %custom-call.62 = f32[1,128,128]{1,2,0:T(8,128)S(1)} custom-call(f32[1,128,128]{2,1,0:T(8,128)S(1)} %get-tuple-element.89), custom_call_target="InvertDiagBlocksLowerTriangular" | custom-call | tf_op jit(solution)/shard_map/jit(cholesky)/cholesky | solution.py:24
  306.5 11.9 %cholesky.244 = f32[128,128]{1,0:T(8,128)S(1)} custom-call(f32[128,128]{1,0:T(8,128)S(1)} %cholesky.584), custom_call_target="Cholesky" | custom-call | tf_op jit(solution)/shard_map/jit(cholesky)/cholesky | solution.py:24
  319.1 9.8 %custom-call.63 = f32[1,128,128]{1,2,0:T(8,128)S(1)} custom-call(f32[1,128,128]{2,1,0:T(8,128)S(1)} %get-tuple-element.86), custom_call_target="InvertDiagBlocksLowerTriangular" | custom-call | tf_op jit(solution)/shard_map/jit(cholesky)/cholesky | solution.py:24
  332.2 11.7 %cholesky.468 = f32[128,128]{1,0:T(8,128)S(1)} custom-call(f32[128,128]{1,0:T(8,128)S(1)} %cholesky.589), custom_call_target="Cholesky" | custom-call | tf_op jit(solution)/shard_map/jit(cholesky)/cholesky | solution.py:24
  345.3 9.8 %custom-call.64 = f32[1,128,128]{1,2,0:T(8,128)S(1)} custom-call(f32[1,128,128]{2,1,0:T(8,128)S(1)} %get-tuple-element.83), custom_call_target="InvertDiagBlocksLowerTriangular" | custom-call | tf_op jit(solution)/shard_map/jit(cholesky)/cholesky | solution.py:24
  358.6 12.1 %cholesky.487 = f32[128,128]{1,0:T(8,128)S(1)} custom-call(f32[128,128]{1,0:T(8,128)S(1)} %cholesky.594), custom_call_target="Cholesky" | custom-call | tf_op jit(solution)/shard_map/jit(cholesky)/cholesky | solution.py:24
  372.0 9.8 %custom-call.65 = f32[1,128,128]{1,2,0:T(8,128)S(1)} custom-call(f32[1,128,128]{2,1,0:T(8,128)S(1)} %get-tuple-element.80), custom_call_target="InvertDiagBlocksLowerTriangular" | custom-call | tf_op jit(solution)/shard_map/jit(cholesky)/cholesky | solution.py:24
  385.3 11.7 %cholesky.506 = f32[128,128]{1,0:T(8,128)S(1)} custom-call(f32[128,128]{1,0:T(8,128)S(1)} %cholesky.599), custom_call_target="Cholesky" | custom-call | tf_op jit(solution)/shard_map/jit(cholesky)/cholesky | solution.py:24
  398.4 9.9 %custom-call.66 = f32[1,128,128]{1,2,0:T(8,128)S(1)} custom-call(f32[1,128,128]{2,1,0:T(8,128)S(1)} %get-tuple-element.77), custom_call_target="InvertDiagBlocksLowerTriangular" | custom-call | tf_op jit(solution)/shard_map/jit(cholesky)/cholesky | solution.py:24
  411.7 11.7 %cholesky.526 = f32[128,128]{1,0:T(8,128)S(1)} custom-call(f32[128,128]{1,0:T(8,128)S(1)} %cholesky.604), custom_call_target="Cholesky" | custom-call | tf_op jit(solution)/shard_map/jit(cholesky)/cholesky | solution.py:24
  424.7 9.8 %custom-call.67 = f32[1,128,128]{1,2,0:T(8,128)S(1)} custom-call(f32[1,128,128]{2,1,0:T(8,128)S(1)} %get-tuple-element.74), custom_call_target="InvertDiagBlocksLowerTriangular" | custom-call | tf_op jit(solution)/shard_map/jit(cholesky)/cholesky | solution.py:24
  437.5 11.9 %cholesky.546 = f32[128,128]{1,0:T(8,128)S(1)} custom-call(f32[128,128]{1,0:T(8,128)S(1)} %cholesky.609), custom_call_target="Cholesky" | custom-call | tf_op jit(solution)/shard_map/jit(cholesky)/cholesky | solution.py:24
  450.7 9.8 %custom-call.68 = f32[1,128,128]{1,2,0:T(8,128)S(1)} custom-call(f32[1,128,128]{2,1,0:T(8,128)S(1)} %get-tuple-element.71), custom_call_target="InvertDiagBlocksLowerTriangular" | custom-call | tf_op jit(solution)/shard_map/jit(cholesky)/cholesky | solution.py:24
  463.2 11.7 %cholesky.564 = f32[128,128]{1,0:T(8,128)S(1)} custom-call(f32[128,128]{1,0:T(8,128)S(1)} %convolution_subtract_fusion.6), custom_call_target="Cholesky" | custom-call | tf_op jit(solution)/shard_map/jit(cholesky)/cholesky | solution.py:24
  482.0 5.0 select_select_fusion
  487.0 23.2 %while.14 = (s32[]{:T(128)}, f32[1024,1024]{1,0:T(8,128)}, s32[8,2]{0,1:T(2,128)S(1)}, f32[8,128,128]{2,1,0:T(8,128)S(1)}, s32[]{:T(128)}) while((s32[]{:T(128)}, f32[1024,1024]{1,0:T(8,128)}, s32[8,2]{0,1:T(2,128)S(1)}, f32[8,128,128]{2,1,0:T(8,128)S(1)}, s32[]{:T(128)}) %tuple.81), condition=%wide.while_cond, body=%wide.while_body.sunk | while | flops 2 | bytes 131189 | solution.py:25
  510.2 78.6 %custom-call.69 = f32[8,128,128]{1,2,0:T(8,128)S(1)} custom-call(f32[8,128,128]{2,1,0:T(8,128)S(1)} %get-tuple-element.40), custom_call_target="InvertDiagBlocksLowerTriangular" | custom-call | tf_op jit(solution)/shard_map/triangular_solve | solution.py:25
  602.4 19.7 %psum.23 = f32[]{:T(128)} all-reduce(f32[]{:T(128)} %fusion.70), channel_id=1, replica_groups=mesh['dp'=8,'seq'=4] {'dp'}, use_global_device_ids=true, to_apply=%region_26.27 | all-reduce | flops 1 | bytes 8 | tf_op jit(solution)/shard_map/psum | solution.py:94
  (161 shorter events, 117.9 us)
Async XLA Ops:
  8.0 1.6 copy-start
  8.0 252.4 %all-reduce.3.cloned.1.call-start = ((), (), s32[]{:S(2)}) async-start(), calls=%async_computation.1 | async-start | bytes 8388608 | tf_op jit(solution)/shard_map/psum | solution.py:92
  12.8 1.7 copy-start.9
  13.1 18.4 %copy-start.3 = (bf16[2,256,16,64]{1,0,3,2:T(2,128)(2,1)}, bf16[2,256,16,64]{1,0,3,2:T(2,128)(2,1)S(1)}, u32[]{:S(2)}) copy-start(bf16[2,256,16,64]{1,0,3,2:T(2,128)(2,1)S(1)} %reshape.179) | copy-start | bytes 3145732
  31.5 1.0 copy-start.6
  32.6 7.7 %collective-permute-start = (f32[2,16,64,64]{3,2,1,0:T(8,128)S(1)}, f32[2,16,64,64]{3,2,1,0:T(8,128)S(1)}, u32[]{:S(2)}, u32[]{:S(2)}) collective-permute-start(f32[2,16,64,64]{3,2,1,0:T(8,128)S(1)} %add.179), channel_id=1, source_target_pairs={{0,1},{1,2},{2,3},{4,5},{5,6},{6,7},{8,9},{9,10},{10,11},{12,13},{... | collective-permute-start | bytes 1572872 | tf_op jit(solution)/shard_map/while/body/eval_jaxpr/ppermute | solution.py:13
  35.1 5.3 collective-permute-start.1
  40.5 16.3 %collective-permute-start = (f32[2,16,64,64]{3,2,1,0:T(8,128)S(1)}, f32[2,16,64,64]{3,2,1,0:T(8,128)S(1)}, u32[]{:S(2)}, u32[]{:S(2)}) collective-permute-start(f32[2,16,64,64]{3,2,1,0:T(8,128)S(1)} %add.179), channel_id=1, source_target_pairs={{0,1},{1,2},{2,3},{4,5},{5,6},{6,7},{8,9},{9,10},{10,11},{12,13},{... | collective-permute-start | bytes 1572872 | tf_op jit(solution)/shard_map/while/body/eval_jaxpr/ppermute | solution.py:13
  51.7 5.2 collective-permute-start.1
  57.0 16.3 %collective-permute-start = (f32[2,16,64,64]{3,2,1,0:T(8,128)S(1)}, f32[2,16,64,64]{3,2,1,0:T(8,128)S(1)}, u32[]{:S(2)}, u32[]{:S(2)}) collective-permute-start(f32[2,16,64,64]{3,2,1,0:T(8,128)S(1)} %add.179), channel_id=1, source_target_pairs={{0,1},{1,2},{2,3},{4,5},{5,6},{6,7},{8,9},{9,10},{10,11},{12,13},{... | collective-permute-start | bytes 1572872 | tf_op jit(solution)/shard_map/while/body/eval_jaxpr/ppermute | solution.py:13
  68.1 5.2 collective-permute-start.1
  73.7 3.4 copy-start.4
  73.7 3.4 copy-start.5
  77.1 1.4 copy-start.7
  79.4 1.4 copy-start.12
  79.4 1.6 copy-start.8
  79.4 1.9 copy-start.10
  82.6 10.0 %collective-permute-start.2 = (f32[2,1024]{1,0:T(2,128)S(1)}, f32[2,1024]{1,0:T(2,128)S(1)}, u32[]{:S(2)}, u32[]{:S(2)}) collective-permute-start(f32[2,1024]{1,0:T(2,128)S(1)} %multiply_reduce_fusion), channel_id=1, source_target_pairs={{0,1},{1,0},{2,3},{3,2},{4,5},{5,4},{6,7},{7,6},{8,9},{9,8},{10,11... | collective-permute-start | bytes 24584 | tf_op jit(solution)/shard_map/ppermute | solution.py:85
  92.6 4.3 collective-permute-start.3
  102.1 158.3 %all-gather.2.cloned.1.call-start = ((), (), s32[]{:S(2)}) async-start(), calls=%async_computation | async-start | bytes 5242880 | tf_op jit(solution)/shard_map/all_gather | solution.py:87
  276.5 2.0 copy-start.2
  482.0 140.8 %copy-start.1 = (bf16[1024,1024]{1,0:T(8,128)(2,1)S(1)}, bf16[1024,1024]{1,0:T(8,128)(2,1)}, u32[]{:S(2)}) copy-start(bf16[1024,1024]{1,0:T(8,128)(2,1)} %param.12) | copy-start | bytes 6291460
  599.3 23.5 %copy-start.11 = (f32[1024,2]{0,1:T(2,128)}, f32[1024,2]{0,1:T(2,128)S(1)}, u32[]{:S(2)}) copy-start(f32[1024,2]{0,1:T(2,128)S(1)} %convolution_dynamic-update-slice_fusion.6) | copy-start | bytes 24580
Sparse Core Ops, SparseCore 0:
  102.3 158.1 all-reduce.2
Sparse Core Ops, SparseCore 1:
  104.2 36.0 all-gather.1
